TPU v7x, 32 devices: a whole 2x2x4 slice. The times are simulated.
32 devices in a mesh: site: 8 (over z, y), mode: 4 (over x, core).
Axes of the slice: x: 2, y: 2, z: 4, core: 2. Of those that a mesh axis runs over, the one named last changes fastest.
Arguments:
- basis: bfloat16 [64, 400, 512], P('site', 'mode'), may hold values from -6 to 6
- images: bfloat16 [64, 400, 496], P('site', 'mode'), may hold values from -6 to 6
- hops: bfloat16 [64, 9, 400, 400], P('site', None, 'mode'), may hold values from -0.09375 to 0.09375
- neighbours: int32 [64, 8], P('site'), may hold values from 0 to 47, as said below
- rotation: bfloat16 [512, 512], replicated, may hold values from -0.25 to 0.25
Outputs:
- projected: float32 [512, 512], replicated
- rotated_basis: bfloat16 [64, 400, 512], P('site', 'mode')
- rotated_images: bfloat16 [64, 400, 512], P('site', 'mode')
Inputs may be any that keep to these rules, and one draw needn't show every extreme that they name: `neighbours`: the blocks form a periodic 4 x 4 x 4 x 64/64 lattice. Group s = 8 t + 4 gx + 2 gy + gz holds the 2 x 2 x 2 cube of time slice t at spatial offsets 2 gx, 2 gy, 2 gz, stored in its own order.
All inputs are finite; a program needn't handle non-finite values.
Results may differ from a plain program's by a relative error of at most 0.0026.
Values may be sent and summed in bfloat16 or wider, within the bound.
No kernel may reach another device: no remote copies, remote signals or barrier semaphores. Data moves between devices by JAX's collectives and lax.ppermute only.
A program may use at most 64 MiB of HBM per device.

v0:
```python
import math
import jax
import jax.numpy as jnp
from jax import lax
from jax.sharding import PartitionSpec as P

OLD = 496


def swapped(block, axis, distance):
    count = lax.axis_size(axis)
    route = []
    for low in range(count):
        high = low | 1 << distance
        if high != low and high < count:
            route += [(low, high), (high, low)]
    return lax.ppermute(block, axis, route)


def from_behind(block, axis, distance):
    devices = range(lax.axis_size(axis))
    route = [((i - distance) % len(devices), i) for i in devices]
    return lax.ppermute(block, axis, route)


def local(basis, images, hops, neighbours, rotation):
    local_blocks = basis.shape[0]
    modes_here = basis.shape[1]
    nvec = basis.shape[2]
    site_count = lax.axis_size("site")
    norm_scale = 1.0 / math.sqrt(site_count * local_blocks * modes_here * lax.axis_size("mode"))
    old_part = jnp.einsum("bci,bcj->ij", basis, images, preferred_element_type=jnp.float32)
    old_sum = lax.psum(old_part, ("site", "mode"))
    newest = jnp.transpose(basis[:, :, OLD:], (0, 2, 1))
    pieces = [newest]
    for bit in (2, 1, 0):
        pieces.append(swapped(newest, "site", bit))
    for offset in (-8, 8):
        if site_count > 8:
            pieces.append(from_behind(newest, "site", offset))
        else:
            pieces.append(newest)
    stacked = jnp.concatenate(pieces, axis=0)
    widened = lax.all_gather(stacked, "mode", axis=2, tiled=True)
    own_rows = jnp.arange(local_blocks, dtype=jnp.int32)
    row_index = jnp.concatenate([own_rows[:, None], neighbours], axis=1)
    gathered = widened[row_index]
    stencil = jnp.einsum("bdoi,bdki->bok", hops, gathered, preferred_element_type=jnp.float32)
    image_new = stencil.astype(jnp.bfloat16)
    images_all = jnp.concatenate([images, image_new], axis=2)
    new_part = jnp.einsum("bci,bck->ik", basis, image_new, preferred_element_type=jnp.float32)
    new_sum = lax.psum(new_part, ("site", "mode"))
    projected = jnp.concatenate([old_sum, new_sum], axis=1) * norm_scale
    flat_basis = basis.reshape(local_blocks * modes_here, nvec)
    flat_images = images_all.reshape(local_blocks * modes_here, nvec)
    rotated_basis = jnp.dot(flat_basis, rotation, preferred_element_type=jnp.float32).astype(
        jnp.bfloat16
    )
    rotated_images = jnp.dot(flat_images, rotation, preferred_element_type=jnp.float32).astype(
        jnp.bfloat16
    )
    return (
        projected,
        rotated_basis.reshape(local_blocks, modes_here, nvec),
        rotated_images.reshape(local_blocks, modes_here, nvec),
    )


def solution(mesh):
    placed = (
        P("site", "mode", None),
        P("site", "mode", None),
        P("site", None, "mode", None),
        P("site", None),
        P(),
    )
    return jax.shard_map(
        local,
        mesh=mesh,
        in_specs=placed,
        out_specs=(P(), P("site", "mode", None), P("site", "mode", None)),
        check_vma=False,
    )
```

profile of v0, /device:TPU:0, one launch (start us, length us, event | category | flops | bytes accessed | tf_op | source)
XLA Modules:
  0.0 156.1 jit_solution(4232743305024800474)
XLA Ops:
  7.2 1.1 slice.3
  8.3 0.2 copy.50
  8.5 4.1 %collective-permute-start = (bf16[8,16,100]{2,1,0:T(8,128)(2,1)S(1)}, bf16[8,16,100]{2,1,0:T(8,128)(2,1)S(1)}, u32[]{:S(2)}, u32[]{:S(2)}) collective-permute-start(bf16[8,16,100]{2,1,0:T(8,128)(2,1)S(1)} %bitcast.32), channel_id=1, source_target_pairs={{0,16},{16,0},{4,20},{20,4},{8,24},{24,8},{12,28},{28,12},{1,17},{... | collective-permute-start | bytes 76808 | tf_op jit(solution)/shard_map/ppermute | solution.py:17
  12.6 1.6 %collective-permute-start.1 = (bf16[8,16,100]{2,1,0:T(8,128)(2,1)S(1)}, bf16[8,16,100]{2,1,0:T(8,128)(2,1)S(1)}, u32[]{:S(2)}, u32[]{:S(2)}) collective-permute-start(bf16[8,16,100]{2,1,0:T(8,128)(2,1)S(1)} %bitcast.33), channel_id=1, source_target_pairs={{0,8},{8,0},{4,12},{12,4},{16,24},{24,16},{20,28},{28,20},{1,9},{9... | collective-permute-start | bytes 76808 | tf_op jit(solution)/shard_map/ppermute | solution.py:17
  14.2 1.5 collective-permute-start.2
  15.7 3.1 %convolution_bitcast_fusion = f32[512,496]{0,1:T(8,128)} fusion(bf16[8,100,512]{2,0,1:T(8,128)(2,1)} %param.5, bf16[8,100,496]{2,0,1:T(8,128)(2,1)} %param.6), kind=kOutput, calls=%fused_computation.5 | convolution fusion | flops 406323200 | bytes 2628608 | tf_op jit(solution)/shard_map/bci,bcj->ij/dot_general | solution.py:32
  18.9 0.2 copy.42
  19.1 0.4 copy-done.4
  19.8 0.6 convolution_convert_fusion.1
  20.6 1.1 copy.47
  21.8 0.4 copy.39
  22.3 14.5 %all_gather.3 = bf16[48,16,400]{0,1,2:T(8,128)(2,1)S(1)} all-gather(bf16[48,16,100]{0,1,2:T(8,128)(2,1)S(1)} %copy.39), channel_id=1, replica_groups=mesh['site'=8,'mode'=4] {'mode'}, dimensions={2}, use_global_device_ids=true | all-gather | bytes 768000 | tf_op jit(solution)/shard_map/all_gather | solution.py:44
  36.7 2.1 %copy.40 = bf16[48,16,400]{2,1,0:T(8,128)(2,1)S(1)} copy(bf16[48,16,400]{0,1,2:T(8,128)(2,1)S(1)} %all_gather.3) | data formatting | bytes 1228800 | tf_op jit(solution)/shard_map/all_gather | solution.py:44
  38.8 0.7 gather_fusion
  39.5 5.3 %fusion.8 = bf16[8,100,16]{1,2,0:T(8,128)(2,1)S(1)} fusion(bf16[8,9,16,400]{3,2,1,0:T(8,128)(2,1)S(1)} %bitcast.31, bf16[8,9,100,400]{3,0,2,1:T(8,128)(2,1)} %param.7), kind=kOutput, calls=%fused_computation.8 | convolution fusion | flops 92172800 | bytes 6707200 | tf_op jit(solution)/shard_map/bdoi,bdki->bok/dot_general | solution.py:48
  44.8 0.2 copy.44
  45.2 0.2 copy.45
  45.6 0.6 convolution_convert_fusion
  46.4 1.1 copy.48
  47.5 0.4 convolution_bitcast_fusion.1
  47.9 38.0 %psum.15 = f32[512,16]{0,1:T(8,128)S(1)} all-reduce(f32[512,16]{0,1:T(8,128)S(1)} %convolution_bitcast_fusion.1), channel_id=1, replica_groups=mesh['site'=8,'mode'=4] {'site','mode'}, use_global_device_ids=true, to_apply=%region_1.0 | all-reduce | flops 8192 | bytes 65536 | tf_op jit(solution)/shard_map/psum | solution.py:52
  85.9 60.7 %all-reduce.2.cloned.1.call-done = f32[512,496]{0,1:T(8,128)} async-done(((f32[512,496]{0,1:T(8,128)}), f32[512,496]{0,1:T(8,128)}) %all-reduce.2.cloned.1.call-update) | async-done | bytes 1015824 | tf_op jit(solution)/shard_map/psum | solution.py:33
  146.6 1.3 maximum_multiply_fusion
  147.9 1.3 copy.46
  (29 shorter events, 1.1 us)
Async XLA Ops:
  7.2 12.7 %copy-start = (bf16[512,512]{1,0:T(8,128)(2,1)S(1)}, bf16[512,512]{1,0:T(8,128)(2,1)}, u32[]{:S(2)}) copy-start(bf16[512,512]{1,0:T(8,128)(2,1)} %param.9) | copy-start | bytes 1572868
  7.2 139.4 %all-reduce.2.cloned.1.call-start = ((), (), s32[]{:S(2)}) async-start(), calls=%async_computation | async-start | bytes 2031616 | tf_op jit(solution)/shard_map/psum | solution.py:33
  8.5 10.3 %copy-start.1 = (bf16[8,100,512]{2,0,1:T(8,128)(2,1)S(1)}, bf16[8,100,512]{2,0,1:T(8,128)(2,1)}, u32[]{:S(2)}) copy-start(bf16[8,100,512]{2,0,1:T(8,128)(2,1)} %param.5) | copy-start | bytes 2457604
  8.5 13.2 %collective-permute-start = (bf16[8,16,100]{2,1,0:T(8,128)(2,1)S(1)}, bf16[8,16,100]{2,1,0:T(8,128)(2,1)S(1)}, u32[]{:S(2)}, u32[]{:S(2)}) collective-permute-start(bf16[8,16,100]{2,1,0:T(8,128)(2,1)S(1)} %bitcast.32), channel_id=1, source_target_pairs={{0,16},{16,0},{4,20},{20,4},{8,24},{24,8},{12,28},{28,12},{1,17},{... | collective-permute-start | bytes 76808 | tf_op jit(solution)/shard_map/ppermute | solution.py:17
  12.6 9.1 %collective-permute-start.1 = (bf16[8,16,100]{2,1,0:T(8,128)(2,1)S(1)}, bf16[8,16,100]{2,1,0:T(8,128)(2,1)S(1)}, u32[]{:S(2)}, u32[]{:S(2)}) collective-permute-start(bf16[8,16,100]{2,1,0:T(8,128)(2,1)S(1)} %bitcast.33), channel_id=1, source_target_pairs={{0,8},{8,0},{4,12},{12,4},{16,24},{24,16},{20,28},{28,20},{1,9},{9... | collective-permute-start | bytes 76808 | tf_op jit(solution)/shard_map/ppermute | solution.py:17
  14.2 7.5 %collective-permute-start.2 = (bf16[8,16,100]{2,1,0:T(8,128)(2,1)S(1)}, bf16[8,16,100]{2,1,0:T(8,128)(2,1)S(1)}, u32[]{:S(2)}, u32[]{:S(2)}) collective-permute-start(bf16[8,16,100]{2,1,0:T(8,128)(2,1)S(1)} %bitcast.34), channel_id=1, source_target_pairs={{0,4},{4,0},{8,12},{12,8},{16,20},{20,16},{24,28},{28,24},{1,5},{5... | collective-permute-start | bytes 76808 | tf_op jit(solution)/shard_map/ppermute | solution.py:17
  18.8 0.7 copy-start.4
  39.5 5.5 %copy-start.3 = (bf16[8,100,496]{2,0,1:T(8,128)(2,1)S(1)}, bf16[8,100,496]{2,0,1:T(8,128)(2,1)}, u32[]{:S(2)}) copy-start(bf16[8,100,496]{2,0,1:T(8,128)(2,1)} %param.6) | copy-start | bytes 2380804
  46.2 1.3 copy-start.2
Sparse Core Ops, SparseCore 0:
  19.0 127.5 all-reduce.1
where the time goes:
time: 156 us
  waiting for transfers between devices  60.7 us (39%)
  blocking collectives  52.5 us (34%)
  between operations  14.2 us (9%)
  matrix products  9.92 us (6%)
  local copies, waits for them, and re-layouts  9.89 us (6%)
  starting transfers between devices  7.26 us (5%)
  other arithmetic  1.57 us (1%)
    psum x1, waiting for transfers between devices, local(): old_sum = lax.psum(old_part, ('site', 'mode'))  60.7 us
    psum x1, blocking collectives, local(): new_sum = lax.psum(new_part, ('site', 'mode'))  38 us
    all_gather x1, blocking collectives, local(): widened = lax.all_gather(stacked, 'mode', axis=2, tiled=True)  14.5 us
    ppermute x3, starting transfers between devices, swapped(): return lax.ppermute(block, axis, route)  7.22 us
    dot_general x1, matrix products, local(): jnp.einsum('bdoi,bdki->bok', hops, gathered, preferred_element_type=jnp.f...  5.31 us
    unnamed x20, local copies, waits for them, and re-layouts  4.45 us
  transfers between devices with their start and end apart: 4, of which 1 were waited for; matrix products, arithmetic and copies ran while one was open for 11% of the time, Pallas kernels for 0%

commit v1 on v0

--- a/solution.py
+++ b/solution.py
@@ -30,7 +30,7 @@
     site_count = lax.axis_size("site")
     norm_scale = 1.0 / math.sqrt(site_count * local_blocks * modes_here * lax.axis_size("mode"))
     old_part = jnp.einsum("bci,bcj->ij", basis, images, preferred_element_type=jnp.float32)
-    old_sum = lax.psum(old_part, ("site", "mode"))
+    old_sum = jnp.sum(lax.all_gather(old_part, ("site", "mode")), axis=0)
     newest = jnp.transpose(basis[:, :, OLD:], (0, 2, 1))
     pieces = [newest]
     for bit in (2, 1, 0):

time: 156 us -> 258 us (1.65)
  waiting for transfers between devices: 60.7 us -> 116 us
  local copies, waits for them, and re-layouts: 9.89 us -> 43.1 us
  blocking collectives: 52.5 us -> 63.6 us
    all_gather x0 -> x1, waiting for transfers between devices: none -> 116 us  [local(): old_sum = jnp.sum(lax.all_gather(old_part, ('site', 'mode')), axis=0)]
    psum x1 -> x0, waiting for transfers between devices: 60.7 us -> none  [local(): old_sum = lax.psum(old_part, ('site', 'mode'))]
    unnamed x20 -> x23, local copies, waits for them, and re-layouts: 4.45 us -> 38.7 us
    all_gather x1, blocking collectives: 14.5 us -> 21.4 us  [local(): widened = lax.all_gather(stacked, 'mode', axis=2, tiled=True)]
    psum x1, blocking collectives: 38 us -> 42.3 us  [local(): new_sum = lax.psum(new_part, ('site', 'mode'))]
    reduce_sum x0 -> x1, other arithmetic: none -> 3.08 us  [local(): old_sum = jnp.sum(lax.all_gather(old_part, ('site', 'mode')), axis=0)]
  transfers between devices with their start and end apart: 4 -> 4, of which waited for: 1 -> 1; matrix products, arithmetic and copies ran while one was open for 11% -> 6% of each run, Pallas kernels for 0% -> 0%
where the time goes in v1:
time: 258 us
  waiting for transfers between devices  116 us (45%)
  blocking collectives  63.6 us (25%)
  local copies, waits for them, and re-layouts  43.1 us (17%)
  between operations  14.3 us (6%)
  matrix products  10 us (4%)
  starting transfers between devices  7.25 us (3%)
  other arithmetic  3.45 us (1%)
    all_gather x1, waiting for transfers between devices, local(): old_sum = jnp.sum(lax.all_gather(old_part, ('site', 'mode')), axis=0)  116 us
    psum x1, blocking collectives, local(): new_sum = lax.psum(new_part, ('site', 'mode'))  42.3 us
    unnamed x23, local copies, waits for them, and re-layouts  38.7 us
    all_gather x1, blocking collectives, local(): widened = lax.all_gather(stacked, 'mode', axis=2, tiled=True)  21.4 us
    ppermute x3, starting transfers between devices, swapped(): return lax.ppermute(block, axis, route)  7.21 us
    dot_general x1, matrix products, local(): jnp.einsum('bdoi,bdki->bok', hops, gathered, preferred_element_type=jnp.f...  5.29 us
  transfers between devices with their start and end apart: 4, of which 1 were waited for; matrix products, arithmetic and copies ran while one was open for 6% of the time, Pallas kernels for 0%

profile of v1, /device:TPU:0, one launch (start us, length us, event | category | flops | bytes accessed | tf_op | source)
XLA Modules:
  0.0 257.5 jit_solution(11283658672276343849)
XLA Ops:
  7.2 3.2 %convolution_bitcast_fusion = f32[512,496]{0,1:T(8,128)} fusion(bf16[8,100,512]{2,0,1:T(8,128)(2,1)} %param.5, bf16[8,100,496]{2,0,1:T(8,128)(2,1)} %param.6), kind=kOutput, calls=%fused_computation.6 | convolution fusion | flops 406323200 | bytes 2628608 | tf_op jit(solution)/shard_map/bci,bcj->ij/dot_general | solution.py:32
  10.6 0.2 copy.50
  10.8 4.1 %collective-permute-start = (bf16[8,16,100]{2,1,0:T(8,128)(2,1)S(1)}, bf16[8,16,100]{2,1,0:T(8,128)(2,1)S(1)}, u32[]{:S(2)}, u32[]{:S(2)}) collective-permute-start(bf16[8,16,100]{2,1,0:T(8,128)(2,1)S(1)} %bitcast.38), channel_id=1, source_target_pairs={{0,16},{16,0},{4,20},{20,4},{8,24},{24,8},{12,28},{28,12},{1,17},{... | collective-permute-start | bytes 76808 | tf_op jit(solution)/shard_map/ppermute | solution.py:17
  14.9 1.6 collective-permute-start.1
  16.5 1.5 collective-permute-start.2
  18.0 0.2 copy.42
  18.6 0.6 convolution_convert_fusion.1
  19.3 1.1 copy.47
  20.6 0.4 copy.39
  21.0 21.4 %all_gather.11 = bf16[48,16,400]{0,1,2:T(8,128)(2,1)S(1)} all-gather(bf16[48,16,100]{0,1,2:T(8,128)(2,1)S(1)} %copy.39), channel_id=1, replica_groups=mesh['site'=8,'mode'=4] {'mode'}, dimensions={2}, use_global_device_ids=true | all-gather | bytes 768000 | tf_op jit(solution)/shard_map/all_gather | solution.py:44
  42.4 2.1 copy.40
  44.5 0.7 gather_fusion
  45.2 5.3 %fusion.8 = bf16[8,100,16]{1,2,0:T(8,128)(2,1)S(1)} fusion(bf16[8,9,16,400]{3,2,1,0:T(8,128)(2,1)S(1)} %bitcast.37, bf16[8,9,100,400]{3,0,2,1:T(8,128)(2,1)} %param.7), kind=kOutput, calls=%fused_computation.9 | convolution fusion | flops 92172800 | bytes 6707200 | tf_op jit(solution)/shard_map/bdoi,bdki->bok/dot_general | solution.py:48
  50.5 0.2 copy.44
  50.7 0.2 pad_maximum_fusion
  50.8 0.2 copy.45
  51.2 0.6 convolution_convert_fusion
  52.0 1.1 copy.48
  53.1 0.4 convolution_bitcast_fusion.1
  53.5 42.3 %psum.7 = f32[512,16]{0,1:T(8,128)S(1)} all-reduce(f32[512,16]{0,1:T(8,128)S(1)} %convolution_bitcast_fusion.1), channel_id=1, replica_groups=mesh['site'=8,'mode'=4] {'site','mode'}, use_global_device_ids=true, to_apply=%region_1.0 | all-reduce | flops 8192 | bytes 65536 | tf_op jit(solution)/shard_map/psum | solution.py:52
  95.8 115.8 %all-gather.3.cloned.1.call-done = f32[16384,496]{0,1:T(8,128)} async-done(((f32[512,496]{0,1:T(8,128)}), f32[16384,496]{0,1:T(8,128)}) %all-gather.3.cloned.1.call-update) | async-done | bytes 32505872 | tf_op jit(solution)/shard_map/all_gather | solution.py:33
  211.6 34.6 %copy.51 = f32[62,8,32,512]{3,2,1,0:T(8,128)S(1)} copy(f32[62,8,32,512]{3,1,2,0:T(8,128)} %bitcast.36) | data formatting | bytes 65011712
  246.2 3.1 %bitcast_reduce_fusion = f32[512,496]{0,1:T(8,128)S(1)} fusion(f32[62,8,32,512]{3,2,1,0:T(8,128)S(1)} %copy.51), kind=kLoop, calls=%fused_computation.1 | loop fusion | flops 7872512 | bytes 33521664 | tf_op jit(solution)/shard_map/reduce_sum | solution.py:33
  249.4 1.3 copy.46
  (33 shorter events, 1.1 us)
Async XLA Ops:
  7.2 11.4 %copy-start = (bf16[512,512]{1,0:T(8,128)(2,1)S(1)}, bf16[512,512]{1,0:T(8,128)(2,1)}, u32[]{:S(2)}) copy-start(bf16[512,512]{1,0:T(8,128)(2,1)} %param.9) | copy-start | bytes 1572868
  7.2 3.3 %copy-start.2 = (bf16[8,100,512]{2,0,1:T(8,128)(2,1)S(1)}, bf16[8,100,512]{2,0,1:T(8,128)(2,1)}, u32[]{:S(2)}) copy-start(bf16[8,100,512]{2,0,1:T(8,128)(2,1)} %param.5) | copy-start | bytes 2457604
  7.2 204.4 %all-gather.3.cloned.1.call-start = ((), (), s32[]{:S(2)}) async-start(), calls=%async_computation | async-start | bytes 33521664 | tf_op jit(solution)/shard_map/all_gather | solution.py:33
  10.4 7.8 %copy-start.5 = (s32[8,8]{1,0:T(8,128)S(1)}, s32[8,8]{1,0:T(8,128)}, u32[]{:S(2)}) copy-start(s32[8,8]{1,0:T(8,128)} %param.8) | copy-start | bytes 772
  10.8 9.7 %collective-permute-start = (bf16[8,16,100]{2,1,0:T(8,128)(2,1)S(1)}, bf16[8,16,100]{2,1,0:T(8,128)(2,1)S(1)}, u32[]{:S(2)}, u32[]{:S(2)}) collective-permute-start(bf16[8,16,100]{2,1,0:T(8,128)(2,1)S(1)} %bitcast.38), channel_id=1, source_target_pairs={{0,16},{16,0},{4,20},{20,4},{8,24},{24,8},{12,28},{28,12},{1,17},{... | collective-permute-start | bytes 76808 | tf_op jit(solution)/shard_map/ppermute | solution.py:17
  14.9 5.6 %collective-permute-start.1 = (bf16[8,16,100]{2,1,0:T(8,128)(2,1)S(1)}, bf16[8,16,100]{2,1,0:T(8,128)(2,1)S(1)}, u32[]{:S(2)}, u32[]{:S(2)}) collective-permute-start(bf16[8,16,100]{2,1,0:T(8,128)(2,1)S(1)} %bitcast.39), channel_id=1, source_target_pairs={{0,8},{8,0},{4,12},{12,4},{16,24},{24,16},{20,28},{28,20},{1,9},{9... | collective-permute-start | bytes 76808 | tf_op jit(solution)/shard_map/ppermute | solution.py:17
  16.5 4.1 %collective-permute-start.2 = (bf16[8,16,100]{2,1,0:T(8,128)(2,1)S(1)}, bf16[8,16,100]{2,1,0:T(8,128)(2,1)S(1)}, u32[]{:S(2)}, u32[]{:S(2)}) collective-permute-start(bf16[8,16,100]{2,1,0:T(8,128)(2,1)S(1)} %bitcast.40), channel_id=1, source_target_pairs={{0,4},{4,0},{8,12},{12,8},{16,20},{20,16},{24,28},{28,24},{1,5},{5... | collective-permute-start | bytes 76808 | tf_op jit(solution)/shard_map/ppermute | solution.py:17
  45.2 5.5 %copy-start.4 = (bf16[8,100,496]{2,0,1:T(8,128)(2,1)S(1)}, bf16[8,100,496]{2,0,1:T(8,128)(2,1)}, u32[]{:S(2)}) copy-start(bf16[8,100,496]{2,0,1:T(8,128)(2,1)} %param.6) | copy-start | bytes 2380804
  51.8 1.3 copy-start.3
  246.2 4.5 %copy-start.1 = (bf16[512,512]{1,0:T(8,128)(2,1)S(1)}, bf16[512,512]{1,0:T(8,128)(2,1)}, u32[]{:S(2)}) copy-start(bf16[512,512]{1,0:T(8,128)(2,1)} %param.9) | copy-start | bytes 1572868
Sparse Core Ops, SparseCore 0:
  11.5 200.0 all-gather.2
